TPU v7x, 1024 devices: a whole 4x8x16 slice. The times are simulated.
1024 devices in a mesh: dp: 32 (over x_lo, z), seq: 32 (over y, x_hi, core).
Axes of the slice: x: 4 (x_hi: 2, x_lo: 2; x = x_hi * 2 + x_lo), y: 8, z: 16, core: 2. Of those that a mesh axis runs over, the one named last changes fastest.
Arguments:
- q_raw: bfloat16 [32, 4096, 2048], P('dp', 'seq'), may hold values from -500 to 500
- key_projection: bfloat16 [32, 4096, 1024], P('dp', 'seq'), may hold values from -500 to 500
- values: bfloat16 [32, 4096, 1024], P('dp', 'seq'), may hold values from -6 to 6
- output_gradient: bfloat16 [32, 4096, 2048], P('dp', 'seq'), may hold values from -20 to 20
- q_gain: float32 [128], replicated, may hold values from 0.5 to 6
- key_norm_gain: float32 [128], replicated, may hold values from 0.5 to 6
- lengths: int32 [32, 16], P('dp'), may hold values from 1 to 1024, 4096 in all within a row
Outputs:
- q_raw_grad: bfloat16 [32, 4096, 2048], P('dp', 'seq')
- k_raw_grad: bfloat16 [32, 4096, 1024], P('dp', 'seq')
- values_grad: bfloat16 [32, 4096, 1024], P('dp', 'seq')
- q_gain_grad: float32 [128], replicated
- key_gain_gradient: float32 [128], replicated
Inputs may be any that keep to these rules, and one draw needn't show every extreme that they name: Each row's 16 lengths sum to 4096; the longest of a row is 1024.
All inputs are finite; a program needn't handle non-finite values.
Results may differ from a plain program's by a relative error of at most 0.04.
The roundings to bfloat16 on the way count: a program that leaves them out, or rounds other values in their place, can miss the bound.
Values may be sent and summed in bfloat16 or wider, within the bound.
No kernel may reach another device: no remote copies, remote signals or barrier semaphores. Data moves between devices by JAX's collectives and lax.ppermute only.
A program may use at most 32 MiB of HBM per device.

v0:
```python
import math

import jax
import jax.numpy as jnp
from jax import lax
from jax.sharding import PartitionSpec as P

QUERY_HEADS = 16
KEY_VALUE_HEADS = 8
HEAD_SIZE = 128
WINDOW = 256
REACH = 2


score_scale = 168.0 ** (-0.5)
norm_eps = 1e-06


def from_behind(block, axis, distance):
    devices = range(lax.axis_size(axis))
    route = [(i - distance, i) for i in devices if i - distance in devices]
    return lax.ppermute(block, axis, route)


def apply_norm(raw, gain, heads):
    raw_values = raw.astype(jnp.float32).reshape(raw.shape[:-1] + (heads, HEAD_SIZE))
    inverse = lax.rsqrt(jnp.mean(raw_values * raw_values, axis=-1, keepdims=True) + norm_eps)
    return (raw_values, inverse, (raw_values * inverse * gain).astype(jnp.bfloat16))


def norm_backward(raw_values, inverse, gain, normed_grad):
    scaled = gain * normed_grad
    inner = jnp.mean(scaled * raw_values, axis=-1, keepdims=True)
    raw_grad = inverse * scaled - raw_values * inverse * inverse * inverse * inner
    gain_grad = jnp.sum((normed_grad * raw_values * inverse).reshape(-1, HEAD_SIZE), axis=0)
    return (raw_grad, gain_grad)


def doc_index(positions, doc_ends):
    return jnp.sum((positions[None, :, None] >= doc_ends[:, None, :]).astype(jnp.int32), axis=-1)


def local(q_raw, key_projection, values, output_gradient, q_gain, key_norm_gain, lengths):
    row_number, token_number, query_width = q_raw.shape
    group_count = QUERY_HEADS // KEY_VALUE_HEADS
    seq_count = lax.axis_size("seq")
    shard_start = lax.axis_index("seq") * token_number
    query_raw, query_inverse, query_normalized = apply_norm(q_raw, q_gain, QUERY_HEADS)
    key_unnormed, key_inverse_norm, key_normalized = apply_norm(
        key_projection, key_norm_gain, KEY_VALUE_HEADS
    )
    value_head_count = values.reshape(row_number, token_number, KEY_VALUE_HEADS, HEAD_SIZE)
    head_gradients = output_gradient.reshape(
        row_number, token_number, KEY_VALUE_HEADS, group_count, HEAD_SIZE
    )
    query_group_count = query_normalized.reshape(
        row_number, token_number, KEY_VALUE_HEADS, group_count, HEAD_SIZE
    )
    fetched = []
    for offset in range(1, REACH + 1):
        if offset == REACH:
            outgoing = (key_normalized[:, 1:], value_head_count[:, 1:])
        else:
            outgoing = (key_normalized, value_head_count)
        fetched.append(from_behind((outgoing[0], outgoing[1]), "seq", offset))
    key_all = jnp.concatenate([pair[0] for pair in reversed(fetched)] + [key_normalized], axis=1)
    value_all = jnp.concatenate(
        [pair[1] for pair in reversed(fetched)] + [value_head_count], axis=1
    )
    key_count = key_all.shape[1]
    doc_ends = jnp.cumsum(lengths, axis=1)
    query_pos = shard_start + jnp.arange(token_number, dtype=jnp.int32)
    key_pos = shard_start - REACH * token_number + 1 + jnp.arange(key_count, dtype=jnp.int32)
    query_doc = doc_index(query_pos, doc_ends)
    key_doc = doc_index(key_pos, doc_ends)
    distance = query_pos[:, None] - key_pos[None, :]
    in_window = (distance >= 0) & (distance < WINDOW) & (key_pos >= 0)[None, :]
    allowed = (query_doc[:, :, None] == key_doc[:, None, :]) & in_window[None]

    def one_head(item):
        query_head, key_head, value_head, grad_head = item
        scores = (
            jnp.einsum("rqgd,rkd->rgqk", query_head, key_head, preferred_element_type=jnp.float32)
            * score_scale
        )
        scores = jnp.where(allowed[:, None], scores, jnp.float32(-1e30))
        row_max = jnp.max(scores, axis=-1, keepdims=True)
        expanded = jnp.exp(scores - row_max)
        probs = expanded / jnp.sum(expanded, axis=-1, keepdims=True)
        probs_low = probs.astype(jnp.bfloat16)
        attended = jnp.einsum(
            "rgqk,rkd->rqgd", probs_low, value_head, preferred_element_type=jnp.float32
        ).astype(jnp.bfloat16)
        delta_rows = jnp.moveaxis(
            jnp.sum(grad_head.astype(jnp.float32) * attended.astype(jnp.float32), axis=-1), 1, -1
        )
        prob_grad = jnp.einsum(
            "rqgd,rkd->rgqk", grad_head, value_head, preferred_element_type=jnp.float32
        )
        score_grad = (probs * (prob_grad - delta_rows[..., None])).astype(jnp.bfloat16)
        query_grad = (
            jnp.einsum("rgqk,rkd->rqgd", score_grad, key_head, preferred_element_type=jnp.float32)
            * score_scale
        )
        key_grad = (
            jnp.einsum("rgqk,rqgd->rkd", score_grad, query_head, preferred_element_type=jnp.float32)
            * score_scale
        )
        value_gradient = jnp.einsum(
            "rgqk,rqgd->rkd", probs_low, grad_head, preferred_element_type=jnp.float32
        )
        return (query_grad, key_grad, value_gradient)

    head_query, head_key, head_value = lax.map(
        one_head,
        (
            jnp.moveaxis(query_group_count, 2, 0),
            jnp.moveaxis(key_all, 2, 0),
            jnp.moveaxis(value_all, 2, 0),
            jnp.moveaxis(head_gradients, 2, 0),
        ),
    )
    query_grad = jnp.moveaxis(head_query, 0, 2)
    key_grad_all = jnp.moveaxis(head_key, 0, 2)
    value_grad_all = jnp.moveaxis(head_value, 0, 2)
    own_start = key_count - token_number
    key_grad = key_grad_all[:, own_start:]
    value_gradient = value_grad_all[:, own_start:]
    for offset in range(1, REACH + 1):
        if offset == REACH:
            begin = 0
            span = token_number - 1
        else:
            begin = (REACH - offset) * token_number - 1
            span = token_number
        sent_key = key_grad_all[:, begin : begin + span].astype(jnp.bfloat16)
        sent_value = value_grad_all[:, begin : begin + span].astype(jnp.bfloat16)
        back_key, back_value = from_behind((sent_key, sent_value), "seq", -offset)
        back_key = back_key.astype(jnp.float32)
        back_value = back_value.astype(jnp.float32)
        if offset == REACH:
            empty_row = jnp.zeros((row_number, 1, KEY_VALUE_HEADS, HEAD_SIZE), jnp.float32)
            back_key = jnp.concatenate([empty_row, back_key], axis=1)
            back_value = jnp.concatenate([empty_row, back_value], axis=1)
        key_grad = key_grad + back_key
        value_gradient = value_gradient + back_value
    query_unnormed_gradient, query_gain_piece = norm_backward(
        query_raw,
        query_inverse,
        q_gain,
        query_grad.reshape(row_number, token_number, QUERY_HEADS, HEAD_SIZE),
    )
    key_unnormed_gradient, key_gain_piece = norm_backward(
        key_unnormed, key_inverse_norm, key_norm_gain, key_grad
    )
    query_gain_sum, key_gain_total = lax.psum((query_gain_piece, key_gain_piece), ("dp", "seq"))
    token_grand_count = row_number * lax.axis_size("dp") * token_number * seq_count
    q_gain_grad = query_gain_sum / math.sqrt(token_grand_count * QUERY_HEADS)
    key_gain_gradient = key_gain_total / math.sqrt(token_grand_count * KEY_VALUE_HEADS)
    return (
        query_unnormed_gradient.reshape(row_number, token_number, QUERY_HEADS * HEAD_SIZE).astype(
            jnp.bfloat16
        ),
        key_unnormed_gradient.reshape(row_number, token_number, KEY_VALUE_HEADS * HEAD_SIZE).astype(
            jnp.bfloat16
        ),
        value_gradient.reshape(row_number, token_number, KEY_VALUE_HEADS * HEAD_SIZE).astype(
            jnp.bfloat16
        ),
        q_gain_grad,
        key_gain_gradient,
    )


def solution(mesh):
    in_specs = (
        P("dp", "seq", None),
        P("dp", "seq", None),
        P("dp", "seq", None),
        P("dp", "seq", None),
        P(),
        P(),
        P("dp", None),
    )
    out_specs = (P("dp", "seq", None), P("dp", "seq", None), P("dp", "seq", None), P(), P())
    return jax.shard_map(local, mesh=mesh, in_specs=in_specs, out_specs=out_specs, check_vma=False)
```

profile of v0, /device:TPU:1, one launch (start us, length us, event | category | flops | bytes accessed | tf_op | source)
XLA Modules:
  0.0 277.6 jit_solution(9563425994582563639)
XLA Ops:
  3.4 6.0 %collective-permute-start.1 = (bf16[1,128,8,128]{1,3,2,0:T(8,128)(2,1)}, bf16[1,128,8,128]{1,3,2,0:T(8,128)(2,1)}, u32[]{:S(2)}, u32[]{:S(2)}) collective-permute-start(bf16[1,128,8,128]{1,3,2,0:T(8,128)(2,1)} %fusion.58), channel_id=1, source_target_pairs={{0,1},{1,2},{2,3},{3,4},{4,5},{5,6},{6,7},{7,8},{8,9},{9,10},{10,1... | collective-permute-start | bytes 786440 | tf_op jit(solution)/shard_map/ppermute | solution.py:22
  9.4 1.8 slice.36
  11.2 3.8 %collective-permute-start = (bf16[1,127,8,128]{1,3,2,0:T(8,128)(2,1)}, bf16[1,127,8,128]{1,3,2,0:T(8,128)(2,1)}, u32[]{:S(2)}, u32[]{:S(2)}) collective-permute-start(bf16[1,127,8,128]{1,3,2,0:T(8,128)(2,1)} %slice.36), channel_id=1, source_target_pairs={{0,2},{1,3},{2,4},{3,5},{4,6},{5,7},{6,8},{7,9},{8,10},{9,11},{10,... | collective-permute-start | bytes 780296 | tf_op jit(solution)/shard_map/ppermute | solution.py:22
  15.9 1.9 collective-permute-start.3
  17.9 1.8 slice.37
  19.7 4.9 %collective-permute-start.2 = (bf16[1,127,8,128]{1,3,2,0:T(8,128)(2,1)}, bf16[1,127,8,128]{1,3,2,0:T(8,128)(2,1)}, u32[]{:S(2)}, u32[]{:S(2)}) collective-permute-start(bf16[1,127,8,128]{1,3,2,0:T(8,128)(2,1)} %slice.37), channel_id=1, source_target_pairs={{0,2},{1,3},{2,4},{3,5},{4,6},{5,7},{6,8},{7,9},{8,10},{9,11},{10,... | collective-permute-start | bytes 780296 | tf_op jit(solution)/shard_map/ppermute | solution.py:22
  30.0 2.4 maximum_bitcast_fusion
  32.4 2.4 maximum_bitcast_fusion.1
  34.8 73.1 %while.15 = (s32[]{:T(128)}, f32[8,1,128,2,128]{2,4,3,1,0:T(8,128)}, f32[8,1,383,128]{2,3,0,1:T(8,128)}, f32[8,1,383,128]{3,2,1,0:T(8,128)}, bf16[8,1,383,128]{2...) while((s32[]{:T(128)}, ...), condition=%wide.region_9.10_spmd.clone, body=%wide.region_5.9_spmd.clone.sunk | while | flops 152464384 | bytes 4892924 | solution.py:114
  42.2 1.7 fusion.111
  60.4 1.7 fusion.111
  67.8 1.7 fusion.113
  69.6 1.7 fusion.111
  78.7 1.7 fusion.111
  87.8 1.7 fusion.111
  95.2 1.7 fusion.113
  97.0 1.7 fusion.111
  104.4 1.7 fusion.113
  106.1 1.7 fusion.111
  112.7 7.3 %collective-permute-start.4 = (bf16[1,128,8,128]{1,3,2,0:T(8,128)(2,1)}, bf16[1,128,8,128]{1,3,2,0:T(8,128)(2,1)}, u32[]{:S(2)}, u32[]{:S(2)}) collective-permute-start(bf16[1,128,8,128]{1,3,2,0:T(8,128)(2,1)} %slice.39), channel_id=1, source_target_pairs={{1,0},{2,1},{3,2},{4,3},{5,4},{6,5},{7,6},{8,7},{9,8},{10,9},{11,1... | collective-permute-start | bytes 786440 | tf_op jit(solution)/shard_map/ppermute | solution.py:22
  121.3 1.9 collective-permute-start.6
  130.5 3.0 %fusion.51 = bf16[1,128,2048]{2,1,0:T(8,128)(2,1)} fusion(f32[1,128,2048]{2,1,0:T(8,128)} %mul.356, f32[1,128,2048]{2,1,0:T(8,128)} %mul.333, f32[1,128,2048]{2,1,0:T(8,128)} %copy.115, f32[2048]{0:T(1024)S(1)} %broadcast_bitcast_fusion, bf16[1,128,2048]{2,1,0:T(8,128)(2,1)S(1)} %copy-done.2), kind=kLoop, calls=%fused_computation.61 | loop fusion | flops 2359296 | bytes 4202496 | tf_op jit(solution)/shard_map/convert_element_type | solution.py:161
  138.7 136.4 %all-reduce.2 = (f32[128]{0:T(128)S(1)}, f32[128]{0:T(128)S(1)}) all-reduce(f32[128]{0:T(128)S(1)} %fusion.55, f32[128]{0:T(128)S(1)} %get-tuple-element.175), channel_id=1, replica_groups=mesh['dp'=32,'seq'=32] {'dp','seq'}, use_global_device_ids=true, to_apply=%region_13.14 | all-reduce | flops 256 | bytes 2048 | tf_op jit(solution)/shard_map/psum | solution.py:156
  275.6 2.1 copy_bitcast_fusion
  (156 shorter events, 83.4 us)
Async XLA Ops:
  0.6 14.5 %copy-start.6 = (bf16[1,128,1024]{2,1,0:T(8,128)(2,1)S(1)}, bf16[1,128,1024]{2,1,0:T(8,128)(2,1)}, u32[]{:S(2)}) copy-start(bf16[1,128,1024]{2,1,0:T(8,128)(2,1)} %param.11) | copy-start | bytes 786436
  0.6 23.9 %copy-start.1 = (bf16[1,128,2048]{2,1,0:T(8,128)(2,1)S(1)}, bf16[1,128,2048]{2,1,0:T(8,128)(2,1)}, u32[]{:S(2)}) copy-start(bf16[1,128,2048]{2,1,0:T(8,128)(2,1)} %param.9) | copy-start | bytes 1572868
  3.4 26.6 %collective-permute-start.1 = (bf16[1,128,8,128]{1,3,2,0:T(8,128)(2,1)}, bf16[1,128,8,128]{1,3,2,0:T(8,128)(2,1)}, u32[]{:S(2)}, u32[]{:S(2)}) collective-permute-start(bf16[1,128,8,128]{1,3,2,0:T(8,128)(2,1)} %fusion.58), channel_id=1, source_target_pairs={{0,1},{1,2},{2,3},{3,4},{4,5},{5,6},{6,7},{7,8},{8,9},{9,10},{10,1... | collective-permute-start | bytes 786440 | tf_op jit(solution)/shard_map/ppermute | solution.py:22
  11.2 18.7 %collective-permute-start = (bf16[1,127,8,128]{1,3,2,0:T(8,128)(2,1)}, bf16[1,127,8,128]{1,3,2,0:T(8,128)(2,1)}, u32[]{:S(2)}, u32[]{:S(2)}) collective-permute-start(bf16[1,127,8,128]{1,3,2,0:T(8,128)(2,1)} %slice.36), channel_id=1, source_target_pairs={{0,2},{1,3},{2,4},{3,5},{4,6},{5,7},{6,8},{7,9},{8,10},{9,11},{10,... | collective-permute-start | bytes 780296 | tf_op jit(solution)/shard_map/ppermute | solution.py:22
  15.9 16.5 %collective-permute-start.3 = (bf16[1,128,8,128]{1,3,2,0:T(8,128)(2,1)}, bf16[1,128,8,128]{1,3,2,0:T(8,128)(2,1)}, u32[]{:S(2)}, u32[]{:S(2)}) collective-permute-start(bf16[1,128,8,128]{1,3,2,0:T(8,128)(2,1)} %bitcast.6), channel_id=1, source_target_pairs={{0,1},{1,2},{2,3},{3,4},{4,5},{5,6},{6,7},{7,8},{8,9},{9,10},{10,1... | collective-permute-start | bytes 786440 | tf_op jit(solution)/shard_map/ppermute | solution.py:22
  19.7 12.7 %collective-permute-start.2 = (bf16[1,127,8,128]{1,3,2,0:T(8,128)(2,1)}, bf16[1,127,8,128]{1,3,2,0:T(8,128)(2,1)}, u32[]{:S(2)}, u32[]{:S(2)}) collective-permute-start(bf16[1,127,8,128]{1,3,2,0:T(8,128)(2,1)} %slice.37), channel_id=1, source_target_pairs={{0,2},{1,3},{2,4},{3,5},{4,6},{5,7},{6,8},{7,9},{8,10},{9,11},{10,... | collective-permute-start | bytes 780296 | tf_op jit(solution)/shard_map/ppermute | solution.py:22
  24.6 0.7 copy-start.9
  25.5 0.7 copy-start.8
  25.7 1.7 copy-start.5
  107.9 3.2 %copy-start.4 = (f32[8,1,383,128]{3,2,1,0:T(8,128)S(1)}, f32[8,1,383,128]{3,2,1,0:T(8,128)}, u32[]{:S(2)}) copy-start(f32[8,1,383,128]{3,2,1,0:T(8,128)} %get-tuple-element.56) | copy-start | bytes 4706308
  111.1 13.4 %copy-start = (f32[8,1,128,2,128]{2,4,3,1,0:T(8,128)S(1)}, f32[8,1,128,2,128]{2,4,3,1,0:T(8,128)}, u32[]{:S(2)}) copy-start(f32[8,1,128,2,128]{2,4,3,1,0:T(8,128)} %get-tuple-element.54) | copy-start | bytes 3145732
  112.7 21.0 %collective-permute-start.4 = (bf16[1,128,8,128]{1,3,2,0:T(8,128)(2,1)}, bf16[1,128,8,128]{1,3,2,0:T(8,128)(2,1)}, u32[]{:S(2)}, u32[]{:S(2)}) collective-permute-start(bf16[1,128,8,128]{1,3,2,0:T(8,128)(2,1)} %slice.39), channel_id=1, source_target_pairs={{1,0},{2,1},{3,2},{4,3},{5,4},{6,5},{7,6},{8,7},{9,8},{10,9},{11,1... | collective-permute-start | bytes 786440 | tf_op jit(solution)/shard_map/ppermute | solution.py:22
  120.0 13.7 %collective-permute-start.5 = (bf16[1,127,8,128]{1,3,2,0:T(8,128)(2,1)}, bf16[1,127,8,128]{1,3,2,0:T(8,128)(2,1)}, u32[]{:S(2)}, u32[]{:S(2)}) collective-permute-start(bf16[1,127,8,128]{1,3,2,0:T(8,128)(2,1)} %slice.40), channel_id=1, source_target_pairs={{2,0},{3,1},{4,2},{5,3},{6,4},{7,5},{8,6},{9,7},{10,8},{11,9},{12,... | collective-permute-start | bytes 780296 | tf_op jit(solution)/shard_map/ppermute | solution.py:22
  121.3 154.3 %collective-permute-start.6 = (bf16[1,128,8,128]{3,1,0,2:T(8,128)(2,1)}, bf16[1,128,8,128]{3,1,0,2:T(8,128)(2,1)}, u32[]{:S(2)}, u32[]{:S(2)}) collective-permute-start(bf16[1,128,8,128]{3,1,0,2:T(8,128)(2,1)} %slice.42), channel_id=1, source_target_pairs={{1,0},{2,1},{3,2},{4,3},{5,4},{6,5},{7,6},{8,7},{9,8},{10,9},{11,1... | collective-permute-start | bytes 786440 | tf_op jit(solution)/shard_map/ppermute | solution.py:22
  123.2 152.3 %collective-permute-start.7 = (bf16[1,127,8,128]{3,1,0,2:T(8,128)(2,1)}, bf16[1,127,8,128]{3,1,0,2:T(8,128)(2,1)}, u32[]{:S(2)}, u32[]{:S(2)}) collective-permute-start(bf16[1,127,8,128]{3,1,0,2:T(8,128)(2,1)} %slice.43), channel_id=1, source_target_pairs={{2,0},{3,1},{4,2},{5,3},{6,4},{7,5},{8,6},{9,7},{10,8},{11,9},{12,... | collective-permute-start | bytes 780296 | tf_op jit(solution)/shard_map/ppermute | solution.py:22
  129.2 1.4 copy-start.2
  133.5 1.4 copy-start.3
  133.5 1.4 copy-start.7
where the time goes:
time: 280 us; the launch traced here: 278 us
  blocking collectives  136 us (49%)
  matrix products  63.2 us (23%)
  starting transfers between devices  28.5 us (10%)
  local copies, waits for them, and re-layouts  25.3 us (9%)
  other arithmetic  23.1 us (8%)
    psum x1, blocking collectives, local(): lax.psum((query_gain_piece, key_gain_piece), ('dp', 'seq'))  136 us
    ppermute x8, starting transfers between devices, from_behind(): return lax.ppermute(block, axis, route)  28.5 us
    dot_general x8, matrix products, one_head(): jnp.einsum('rgqk,rkd->rqgd', score_grad, key_head, preferred_element_type...  13.8 us
    dot_general x8, matrix products, one_head(): jnp.einsum('rgqk,rqgd->rkd', probs_low, grad_head, preferred_element_type...  13.8 us
    dot_general x8, matrix products, one_head(): jnp.einsum('rqgd,rkd->rgqk', query_head, key_head, preferred_element_type...  9.28 us
    dot_general x8, matrix products, one_head(): jnp.einsum('rqgd,rkd->rgqk', grad_head, value_head, preferred_element_typ...  9.15 us
    dot_general x8, matrix products, one_head(): jnp.einsum('rgqk,rkd->rqgd', probs_low, value_head, preferred_element_typ...  8.78 us
    dot_general x8, matrix products, one_head(): jnp.einsum('rgqk,rqgd->rkd', score_grad, query_head, preferred_element_ty...  8.4 us
  transfers between devices with their start and end apart: 8, of which 0 were waited for; matrix products, arithmetic and copies ran while one was open for 9% of the time, Pallas kernels for 0%

commit v1 on v0

v1 whole, which is shorter than its diff:
```python
import math

import jax
import jax.numpy as jnp
from jax import lax
from jax.experimental import pallas as pl
from jax.experimental.pallas import tpu as pltpu
from jax.sharding import PartitionSpec as P

QUERY_HEADS = 16
KEY_VALUE_HEADS = 8
HEAD_SIZE = 128
WINDOW = 256
REACH = 2
NDOC = 16

score_scale = 168.0 ** (-0.5)
norm_eps = 1e-06
log2_e = 1.4426950408889634

NT = (((1,), (1,)), ((), ()))
NN = (((1,), (0,)), ((), ()))
TN = (((0,), (0,)), ((), ()))


def shift(block, distance):
    count = lax.axis_size("seq")
    route = [(i, i + distance) for i in range(count) if 0 <= i + distance < count]
    return lax.ppermute(block, "seq", route)


def fold_rows(x):
    return jnp.sum(x.reshape(-1, 8, x.shape[-1]), axis=0)


def attention_kernel(
    start_ref,
    lengths_ref,
    q_ref,
    grad_ref,
    key_ref,
    value_ref,
    near_ref,
    far_ref,
    q_gain_ref,
    key_gain_ref,
    q_out_ref,
    key_own_ref,
    value_own_ref,
    near_out_ref,
    far_out_ref,
    gains_ref,
):
    head = pl.program_id(0)
    tokens = q_ref.shape[0]
    groups = q_ref.shape[1] // HEAD_SIZE
    start = start_ref[0]

    def split(ref):
        whole = ref[...]
        return jnp.concatenate(
            [whole[:, g * HEAD_SIZE : (g + 1) * HEAD_SIZE] for g in range(groups)], axis=0
        )

    q_gain = q_gain_ref[...]
    key_gain = key_gain_ref[...]
    q_raw = split(q_ref).astype(jnp.float32)
    q_inverse = lax.rsqrt(jnp.mean(q_raw * q_raw, axis=-1, keepdims=True) + norm_eps)
    q_unit = q_raw * q_inverse
    q_norm = (q_unit * q_gain).astype(jnp.bfloat16)
    grad = split(grad_ref)
    key_raw = jnp.concatenate([far_ref[0], near_ref[0], key_ref[...]], axis=0).astype(jnp.float32)
    key_inverse = lax.rsqrt(jnp.mean(key_raw * key_raw, axis=-1, keepdims=True) + norm_eps)
    key_unit = key_raw * key_inverse
    key_norm = (key_unit * key_gain).astype(jnp.bfloat16)
    values = jnp.concatenate([far_ref[1], near_ref[1], value_ref[...]], axis=0)

    query_pos = start + lax.broadcasted_iota(jnp.int32, (1, tokens), 1)
    first = jnp.maximum(query_pos - (WINDOW - 1), 0)
    end = jnp.int32(0)
    for c in range(NDOC):
        end = end + lengths_ref[0, c]
        first = jnp.maximum(first, jnp.where(query_pos >= end, end, 0))
    first = jnp.concatenate([first] * groups, axis=1)
    last = jnp.concatenate([query_pos] * groups, axis=1)
    key_pos = (
        start - REACH * tokens + lax.broadcasted_iota(jnp.int32, (3 * tokens, groups * tokens), 0)
    )
    allowed = (key_pos >= first) & (key_pos <= last)

    scores = lax.dot_general(key_norm, q_norm, NT, preferred_element_type=jnp.float32)
    scores = jnp.where(allowed, scores, jnp.float32(-1e30))
    top = jnp.max(scores, axis=0, keepdims=True)
    expanded = jnp.exp2((scores - top) * (score_scale * log2_e))
    probs = expanded * (1.0 / jnp.sum(expanded, axis=0, keepdims=True))
    probs_low = probs.astype(jnp.bfloat16)
    prob_grad = lax.dot_general(values, grad, NT, preferred_element_type=jnp.float32)
    delta = jnp.sum(probs * prob_grad, axis=0, keepdims=True)
    score_grad = (probs * (prob_grad - delta)).astype(jnp.bfloat16)

    value_part = lax.dot_general(probs_low, grad, NN, preferred_element_type=jnp.float32)
    key_part = (
        lax.dot_general(score_grad, q_norm, NN, preferred_element_type=jnp.float32) * score_scale
    )
    q_grad = (
        lax.dot_general(score_grad, key_norm, TN, preferred_element_type=jnp.float32) * score_scale
    )

    scaled = q_gain * q_grad
    inner = jnp.mean(scaled * q_raw, axis=-1, keepdims=True)
    q_out = (
        q_inverse * scaled - q_raw * (q_inverse * q_inverse * q_inverse * inner)
    ).astype(jnp.bfloat16)
    for g in range(groups):
        q_out_ref[:, g * HEAD_SIZE : (g + 1) * HEAD_SIZE] = q_out[g * tokens : (g + 1) * tokens]

    far_key = key_part[:tokens].astype(jnp.bfloat16)
    near_key = key_part[tokens : 2 * tokens].astype(jnp.bfloat16)
    own_key = key_part[2 * tokens :]
    far_out_ref[0] = far_key
    near_out_ref[0] = near_key
    key_own_ref[...] = own_key
    far_out_ref[1] = value_part[:tokens].astype(jnp.bfloat16)
    near_out_ref[1] = value_part[tokens : 2 * tokens].astype(jnp.bfloat16)
    value_own_ref[...] = value_part[2 * tokens :]

    q_piece = fold_rows(q_grad * q_unit)
    key_piece = fold_rows(
        far_key.astype(jnp.float32) * key_unit[:tokens]
        + near_key.astype(jnp.float32) * key_unit[tokens : 2 * tokens]
        + own_key * key_unit[2 * tokens :]
    )
    pieces = jnp.concatenate(
        [
            jnp.sum(q_piece, axis=0, keepdims=True),
            jnp.sum(key_piece, axis=0, keepdims=True),
        ],
        axis=0,
    )

    @pl.when(head == 0)
    def _():
        gains_ref[...] = pieces

    @pl.when(head != 0)
    def _():
        gains_ref[...] += pieces


def finish_kernel(
    key_ref, key_own_ref, value_own_ref, near_ref, far_ref, gain_ref, key_out_ref, value_out_ref
):
    gain = gain_ref[...]
    heads = key_ref.shape[1] // HEAD_SIZE
    for h in range(heads):
        at = slice(h * HEAD_SIZE, (h + 1) * HEAD_SIZE)
        total = (
            key_own_ref[:, at]
            + near_ref[0, :, at].astype(jnp.float32)
            + far_ref[0, :, at].astype(jnp.float32)
        )
        raw = key_ref[:, at].astype(jnp.float32)
        inverse = lax.rsqrt(jnp.mean(raw * raw, axis=-1, keepdims=True) + norm_eps)
        scaled = gain * total
        inner = jnp.mean(scaled * raw, axis=-1, keepdims=True)
        key_out_ref[:, at] = (
            inverse * scaled - raw * (inverse * inverse * inverse * inner)
        ).astype(jnp.bfloat16)
    value_out_ref[...] = (
        value_own_ref[...] + near_ref[1].astype(jnp.float32) + far_ref[1].astype(jnp.float32)
    ).astype(jnp.bfloat16)


def attention(start, lengths, q_raw, grad, key_raw, values, near, far, q_gain, key_gain):
    tokens, key_width = key_raw.shape
    heads = key_width // HEAD_SIZE
    wide = q_raw.shape[1] // heads
    smem = pl.BlockSpec(memory_space=pltpu.SMEM)
    by_head = pl.BlockSpec((tokens, HEAD_SIZE), lambda h: (0, h))
    by_group = pl.BlockSpec((tokens, wide), lambda h: (0, h))
    pair = pl.BlockSpec((2, tokens, HEAD_SIZE), lambda h: (0, 0, h))
    row = pl.BlockSpec((1, HEAD_SIZE), lambda h: (0, 0))
    pair_shape = jax.ShapeDtypeStruct((2, tokens, key_width), jnp.bfloat16)
    own_shape = jax.ShapeDtypeStruct((tokens, key_width), jnp.float32)
    flops = 2 * 5 * 3 * tokens * tokens * q_raw.shape[1]
    return pl.pallas_call(
        attention_kernel,
        grid=(heads,),
        in_specs=[smem, smem, by_group, by_group, by_head, by_head, pair, pair, row, row],
        out_specs=[
            by_group,
            by_head,
            by_head,
            pair,
            pair,
            pl.BlockSpec((2, HEAD_SIZE), lambda h: (0, 0)),
        ],
        out_shape=[
            jax.ShapeDtypeStruct(q_raw.shape, jnp.bfloat16),
            own_shape,
            own_shape,
            pair_shape,
            pair_shape,
            jax.ShapeDtypeStruct((2, HEAD_SIZE), jnp.float32),
        ],
        cost_estimate=pl.CostEstimate(
            flops=flops, bytes_accessed=12 * tokens * q_raw.shape[1], transcendentals=0
        ),
        name="window_attention",
    )(start, lengths, q_raw, grad, key_raw, values, near, far, q_gain, key_gain)


def finish(key_raw, key_own, value_own, near, far, key_gain):
    tokens, key_width = key_raw.shape
    blocks = 4
    wide = key_width // blocks
    flat = pl.BlockSpec((tokens, wide), lambda h: (0, h))
    pair = pl.BlockSpec((2, tokens, wide), lambda h: (0, 0, h))
    row = pl.BlockSpec((1, HEAD_SIZE), lambda h: (0, 0))
    shape = jax.ShapeDtypeStruct((tokens, key_width), jnp.bfloat16)
    return pl.pallas_call(
        finish_kernel,
        grid=(blocks,),
        in_specs=[flat, flat, flat, pair, pair, row],
        out_specs=[flat, flat],
        out_shape=[shape, shape],
        cost_estimate=pl.CostEstimate(
            flops=20 * tokens * key_width,
            bytes_accessed=22 * tokens * key_width,
            transcendentals=0,
        ),
        name="finish_keys",
    )(key_raw, key_own, value_own, near, far, key_gain)


def local(q_raw, key_projection, values, output_gradient, q_gain, key_norm_gain, lengths):
    rows, tokens, query_width = q_raw.shape
    seq_count = lax.axis_size("seq")
    start = (lax.axis_index("seq") * tokens).astype(jnp.int32).reshape(1)
    key_raw, value = key_projection[0], values[0]
    key_gain = key_norm_gain.reshape(1, HEAD_SIZE)

    both = jnp.stack([key_raw, value])
    far = shift(both, 2)
    near = shift(both, 1)
    q_out, key_own, value_own, near_part, far_part, gains = attention(
        start,
        lengths,
        q_raw[0],
        output_gradient[0],
        key_raw,
        value,
        near,
        far,
        q_gain.reshape(1, HEAD_SIZE),
        key_gain,
    )
    far_back = shift(far_part, -2)
    near_back = shift(near_part, -1)
    gains = lax.psum(gains, ("dp", "seq"))
    key_out, value_out = finish(key_raw, key_own, value_own, near_back, far_back, key_gain)
    token_total = rows * lax.axis_size("dp") * tokens * seq_count
    return (
        q_out[None],
        key_out[None],
        value_out[None],
        gains[0] / math.sqrt(token_total * QUERY_HEADS),
        gains[1] / math.sqrt(token_total * KEY_VALUE_HEADS),
    )


def solution(mesh):
    by_token = P("dp", "seq", None)
    in_specs = (by_token, by_token, by_token, by_token, P(), P(), P("dp", None))
    out_specs = (by_token, by_token, by_token, P(), P())
    return jax.shard_map(local, mesh=mesh, in_specs=in_specs, out_specs=out_specs, check_vma=False)
```

time: 280 us -> 190 us (0.68)
  matrix products: 63.2 us -> 0 us
  other arithmetic: 23.1 us -> 0.52 us
  local copies, waits for them, and re-layouts: 25.3 us -> 2.85 us
  Pallas kernels: 0 us -> 13.5 us
  starting transfers between devices: 28.5 us -> 17.8 us
  waiting for transfers between devices: 0.02 us -> 8.74 us
  blocking collectives: 136 us -> 144 us
    dot_general x48 -> x0, matrix products: 63.2 us -> none  [the longest x8 13.8 us: one_head(): jnp.einsum('rgqk,rkd->rqgd', score_grad, key_head, preferred_element_type...]
    pallas_call x0 -> x2, Pallas kernels: none -> 13.5 us  [the longest x1 9.7 us: attention(): pl.pallas_call(attention_kernel, grid=(heads,), in_specs=[smem, smem, by_...]
    ppermute x8 -> x4, starting transfers between devices: 28.5 us -> 17.8 us  [shift(): return lax.ppermute(block, 'seq', route)]
    ppermute x8 -> x4, waiting for transfers between devices: 0.02 us -> 8.74 us  [shift(): return lax.ppermute(block, 'seq', route)]
    convert_element_type x12 -> x0, other arithmetic: 8.48 us -> none  [the longest x1 2.99 us: local(): query_unnormed_gradient.reshape(row_number, token_number, QUERY_HEADS * H...]
    psum x1, blocking collectives: 136 us -> 144 us  [local(): gains = lax.psum(gains, ('dp', 'seq'))]
    slice x6 -> x0, local copies, waits for them, and re-layouts: 6.71 us -> none  [the longest x2 3.6 us: local(): outgoing = (key_normalized[:, 1:], value_head_count[:, 1:])]
    dynamic_update_slice x16 -> x0, local copies, waits for them, and re-layouts: 6.58 us -> none  [local(): lax.map(one_head, (jnp.moveaxis(query_group_count, 2, 0), jnp.moveaxis(ke...]
  transfers between devices with their start and end apart: 8 -> 4, of which waited for: 0 -> 2; matrix products, arithmetic and copies ran while one was open for 9% -> 0% of each run, Pallas kernels for 0% -> 0%
where the time goes in v1:
time: 190 us; the launch traced here: 188 us
  blocking collectives  144 us (76%)
  starting transfers between devices  17.8 us (9%)
  Pallas kernels  13.5 us (7%)
  waiting for transfers between devices  8.74 us (5%)
  local copies, waits for them, and re-layouts  2.85 us (2%)
    psum x1, blocking collectives, local(): gains = lax.psum(gains, ('dp', 'seq'))  144 us
    ppermute x4, starting transfers between devices, shift(): return lax.ppermute(block, 'seq', route)  17.8 us
    pallas_call x1, Pallas kernels, attention(): pl.pallas_call(attention_kernel, grid=(heads,), in_specs=[smem, smem, by_...  9.7 us
    ppermute x4, waiting for transfers between devices, shift(): return lax.ppermute(block, 'seq', route)  8.74 us
    pallas_call x1, Pallas kernels, finish(): pl.pallas_call(finish_kernel, grid=(blocks,), in_specs=[flat, flat, flat,...  3.84 us
  transfers between devices with their start and end apart: 4, of which 2 were waited for; matrix products, arithmetic and copies ran while one was open for 0% of the time, Pallas kernels for 0%

profile of v1, /device:TPU:1, one launch (start us, length us, event | category | flops | bytes accessed | tf_op | source)
XLA Modules:
  0.0 188.2 jit_solution(8714570180175776978)
XLA Ops:
  0.6 0.0 copy-start.2
  0.6 1.0 constant_dynamic-update-slice_fusion.1
  1.7 0.0 copy-done.2
  1.7 5.5 %collective-permute-start.1 = (bf16[2,128,1024]{2,1,0:T(8,128)(2,1)S(1)}, bf16[2,128,1024]{2,1,0:T(8,128)(2,1)S(1)}, u32[]{:S(2)}, u32[]{:S(2)}) collective-permute-start(bf16[2,128,1024]{2,1,0:T(8,128)(2,1)S(1)} %constant_dynamic-update-slice_fusion), channel_id=1, source_target_pairs={{0,2},{1,3},{2,4},{3,5},{4,6},{5,7},{6,8},{7,9},{8,10},{9,11},{10,... | collective-permute-start | bytes 1572872 | tf_op jit(solution)/shard_map/ppermute | solution.py:29
  7.2 4.0 %collective-permute-start = (bf16[2,128,1024]{2,1,0:T(8,128)(2,1)S(1)}, bf16[2,128,1024]{2,1,0:T(8,128)(2,1)S(1)}, u32[]{:S(2)}, u32[]{:S(2)}) collective-permute-start(bf16[2,128,1024]{2,1,0:T(8,128)(2,1)S(1)} %constant_dynamic-update-slice_fusion), channel_id=1, source_target_pairs={{0,1},{1,2},{2,3},{3,4},{4,5},{5,6},{6,7},{7,8},{8,9},{9,10},{10,1... | collective-permute-start | bytes 1572872 | tf_op jit(solution)/shard_map/ppermute | solution.py:29
  11.2 2.1 %collective-permute-done.1.far_ref = bf16[2,128,1024]{2,1,0:T(8,128)(2,1)S(1)} collective-permute-done((bf16[2,128,1024]{2,1,0:T(8,128)(2,1)S(1)}, bf16[2,128,1024]{2,1,0:T(8,128)(2,1)S(1)}, u32[]{:S(2)}, u32[]{:S(2)}) %collective-permute-start.1) | collective-permute-done | bytes 524320 | tf_op jit(solution)/shard_map/ppermute | solution.py:29
  13.3 0.0 copy-start.4
  13.3 6.6 %collective-permute-done.near_ref = bf16[2,128,1024]{2,1,0:T(8,128)(2,1)S(1)} collective-permute-done((bf16[2,128,1024]{2,1,0:T(8,128)(2,1)S(1)}, bf16[2,128,1024]{2,1,0:T(8,128)(2,1)S(1)}, u32[]{:S(2)}, u32[]{:S(2)}) %collective-permute-start) | collective-permute-done | bytes 524320 | tf_op jit(solution)/shard_map/ppermute | solution.py:29
  19.9 0.0 copy-start.5
  19.9 0.0 copy-done.4
  19.9 0.8 copy-done.5
  20.7 9.7 %window_attention.1 = (bf16[128,2048]{1,0:T(8,128)(2,1)}, f32[128,1024]{1,0:T(8,128)}, f32[128,1024]{1,0:T(8,128)}, bf16[2,128,1024]{2,1,0:T(8,128)(2,1)}, bf16[...) custom-call(s32[1]{0:T(128)} %bitcast.start_ref, s32[1,16]{1,0:T(1,128)} %lengths_ref.1, bf16[128,2048]{1,0:T(8,128)(2,1)} %bitcast.19, ...), custom_call_target="tpu_custom_call" | custom-call | flops 1006632960 | bytes 3145728 | tf_op jit(solution)/shard_map/window_attention/pallas_call | solution.py:186
  30.4 7.1 %collective-permute-start.2 = (bf16[2,128,1024]{2,1,0:T(8,128)(2,1)}, bf16[2,128,1024]{2,1,0:T(8,128)(2,1)S(1)}, u32[]{:S(2)}, u32[]{:S(2)}) collective-permute-start(bf16[2,128,1024]{2,1,0:T(8,128)(2,1)} %get-tuple-element.16), channel_id=1, source_target_pairs={{1,0},{2,1},{3,2},{4,3},{5,4},{6,5},{7,6},{8,7},{9,8},{10,9},{11,1... | collective-permute-start | bytes 1572872 | tf_op jit(solution)/shard_map/ppermute | solution.py:29
  37.5 0.0 copy-start.3
  37.5 1.3 collective-permute-start.3
  38.8 0.0 copy-done.3
  38.8 144.0 %psum.7 = f32[2,128]{1,0:T(2,128)S(1)} all-reduce(f32[2,128]{1,0:T(2,128)S(1)} %copy-done.3), channel_id=1, replica_groups=mesh['dp'=32,'seq'=32] {'dp','seq'}, use_global_device_ids=true, to_apply=%region_0.0 | all-reduce | flops 256 | bytes 2048 | tf_op jit(solution)/shard_map/psum | solution.py:260
  182.8 0.5 multiply_bitcast_fusion
  183.3 0.0 collective-permute-done.2.near_ref
  183.3 0.0 collective-permute-done.3.far_ref
  183.3 0.0 copy-start.1
  183.4 0.8 copy-done
  184.1 0.2 copy-done.1
  184.4 3.8 %finish_keys.1 = (bf16[128,1024]{1,0:T(8,128)(2,1)}, bf16[128,1024]{1,0:T(8,128)(2,1)}) custom-call(bf16[128,1024]{1,0:T(8,128)(2,1)} %bitcast.15, f32[128,1024]{1,0:T(8,128)} %get-tuple-element.14.key_own_ref, f32[128,1024]{1,0:T(8,128)} %get-tuple-element.15.value_own_ref, bf16[2,128,1024]{2,1,0:T(8,128)(2,1)} %copy-done, bf16[2,128,1024]{2,1,0:T(8,128)(2,1)} %copy-done.1, ...), custom_call_target="tpu_custom_call" | custom-call | flops 2621440 | bytes 2883584 | tf_op jit(solution)/shard_map/finish_keys/pallas_call | solution.py:221
  (2 shorter events, 0.0 us)
Async XLA Ops:
  0.6 1.0 copy-start.2
  1.7 11.6 %collective-permute-start.1 = (bf16[2,128,1024]{2,1,0:T(8,128)(2,1)S(1)}, bf16[2,128,1024]{2,1,0:T(8,128)(2,1)S(1)}, u32[]{:S(2)}, u32[]{:S(2)}) collective-permute-start(bf16[2,128,1024]{2,1,0:T(8,128)(2,1)S(1)} %constant_dynamic-update-slice_fusion), channel_id=1, source_target_pairs={{0,2},{1,3},{2,4},{3,5},{4,6},{5,7},{6,8},{7,9},{8,10},{9,11},{10,... | collective-permute-start | bytes 1572872 | tf_op jit(solution)/shard_map/ppermute | solution.py:29
  7.2 12.7 %collective-permute-start = (bf16[2,128,1024]{2,1,0:T(8,128)(2,1)S(1)}, bf16[2,128,1024]{2,1,0:T(8,128)(2,1)S(1)}, u32[]{:S(2)}, u32[]{:S(2)}) collective-permute-start(bf16[2,128,1024]{2,1,0:T(8,128)(2,1)S(1)} %constant_dynamic-update-slice_fusion), channel_id=1, source_target_pairs={{0,1},{1,2},{2,3},{3,4},{4,5},{5,6},{6,7},{7,8},{8,9},{9,10},{10,1... | collective-permute-start | bytes 1572872 | tf_op jit(solution)/shard_map/ppermute | solution.py:29
  13.3 6.6 %copy-start.4 = (bf16[2,128,1024]{2,1,0:T(8,128)(2,1)}, bf16[2,128,1024]{2,1,0:T(8,128)(2,1)S(1)}, u32[]{:S(2)}) copy-start(bf16[2,128,1024]{2,1,0:T(8,128)(2,1)S(1)} %collective-permute-done.1.far_ref) | copy-start | bytes 1572868
  19.9 0.8 copy-start.5
  30.4 152.9 %collective-permute-start.2 = (bf16[2,128,1024]{2,1,0:T(8,128)(2,1)}, bf16[2,128,1024]{2,1,0:T(8,128)(2,1)S(1)}, u32[]{:S(2)}, u32[]{:S(2)}) collective-permute-start(bf16[2,128,1024]{2,1,0:T(8,128)(2,1)} %get-tuple-element.16), channel_id=1, source_target_pairs={{1,0},{2,1},{3,2},{4,3},{5,4},{6,5},{7,6},{8,7},{9,8},{10,9},{11,1... | collective-permute-start | bytes 1572872 | tf_op jit(solution)/shard_map/ppermute | solution.py:29
  37.5 1.3 copy-start.3
  37.5 145.8 %collective-permute-start.3 = (bf16[2,128,1024]{2,1,0:T(8,128)(2,1)}, bf16[2,128,1024]{2,1,0:T(8,128)(2,1)S(1)}, u32[]{:S(2)}, u32[]{:S(2)}) collective-permute-start(bf16[2,128,1024]{2,1,0:T(8,128)(2,1)} %get-tuple-element.17), channel_id=1, source_target_pairs={{2,0},{3,1},{4,2},{5,3},{6,4},{7,5},{8,6},{9,7},{10,8},{11,9},{12,... | collective-permute-start | bytes 1572872 | tf_op jit(solution)/shard_map/ppermute | solution.py:29
  183.3 0.8 copy-start
  183.3 1.0 copy-start.1

commit v2 on v1

v2 whole, which is shorter than its diff:
```python
import math

import jax
import jax.numpy as jnp
from jax import lax
from jax.experimental import pallas as pl
from jax.experimental.pallas import tpu as pltpu
from jax.sharding import PartitionSpec as P

QUERY_HEADS = 16
KEY_VALUE_HEADS = 8
HEAD_SIZE = 128
WINDOW = 256
REACH = 2
NDOC = 16
HEADS_PER_STEP = 4
VMEM_LIMIT = 24 << 20
FINISH_LIMIT = 8 << 20
SPREAD_FLOPS = 50_000_000_000

score_scale = 168.0 ** (-0.5)
norm_eps = 1e-06
log2_e = 1.4426950408889634

NT = (((1,), (1,)), ((), ()))
NN = (((1,), (0,)), ((), ()))
TN = (((0,), (0,)), ((), ()))


def shift(block, distance):
    count = lax.axis_size("seq")
    route = [(i, i + distance) for i in range(count) if 0 <= i + distance < count]
    return lax.ppermute(block, "seq", route)


def fold_rows(x):
    return jnp.sum(x.reshape(-1, 8, x.shape[-1]), axis=0)


def attention_kernel(
    lengths_ref,
    q_ref,
    grad_ref,
    key_ref,
    value_ref,
    near_ref,
    far_ref,
    q_gain_ref,
    key_gain_ref,
    q_out_ref,
    key_own_ref,
    value_own_ref,
    near_out_ref,
    far_out_ref,
    terms_ref,
    gains_ref,
):
    step = pl.program_id(0)
    tokens, width = key_ref.shape
    groups = q_ref.shape[1] // width
    start = lax.axis_index("seq") * tokens
    q_gain = q_gain_ref[...]
    key_gain = key_gain_ref[...]

    query_pos = start + lax.broadcasted_iota(jnp.int32, (1, tokens), 1)
    first = jnp.maximum(query_pos - (WINDOW - 1), 0)
    end = jnp.int32(0)
    for c in range(NDOC):
        end = end + lengths_ref[0, c]
        first = jnp.maximum(first, jnp.where(query_pos >= end, end, 0))
    first = jnp.concatenate([first] * groups, axis=1)
    last = jnp.concatenate([query_pos] * groups, axis=1)
    key_pos = (
        start - REACH * tokens + lax.broadcasted_iota(jnp.int32, (3 * tokens, groups * tokens), 0)
    )
    allowed = (key_pos >= first) & (key_pos <= last)

    def one_head(head):
        at = slice(head * HEAD_SIZE, (head + 1) * HEAD_SIZE)
        q_at = [
            slice((head * groups + g) * HEAD_SIZE, (head * groups + g + 1) * HEAD_SIZE)
            for g in range(groups)
        ]
        q_raw = jnp.concatenate([q_ref[:, a] for a in q_at], axis=0).astype(jnp.float32)
        q_inverse = lax.rsqrt(jnp.mean(q_raw * q_raw, axis=-1, keepdims=True) + norm_eps)
        q_unit = q_raw * q_inverse
        q_norm = (q_unit * q_gain).astype(jnp.bfloat16)
        grad = jnp.concatenate([grad_ref[:, a] for a in q_at], axis=0)
        key_raw = jnp.concatenate(
            [far_ref[0, :, at], near_ref[0, :, at], key_ref[:, at]], axis=0
        ).astype(jnp.float32)
        key_inverse = lax.rsqrt(jnp.mean(key_raw * key_raw, axis=-1, keepdims=True) + norm_eps)
        key_unit = key_raw * key_inverse
        key_norm = (key_unit * key_gain).astype(jnp.bfloat16)
        values = jnp.concatenate([far_ref[1, :, at], near_ref[1, :, at], value_ref[:, at]], axis=0)

        scores = lax.dot_general(key_norm, q_norm, NT, preferred_element_type=jnp.float32)
        scores = jnp.where(allowed, scores, jnp.float32(-1e30))
        top = jnp.max(scores, axis=0, keepdims=True)
        expanded = jnp.exp2((scores - top) * (score_scale * log2_e))
        probs = expanded * (1.0 / jnp.sum(expanded, axis=0, keepdims=True))
        probs_low = probs.astype(jnp.bfloat16)
        prob_grad = lax.dot_general(values, grad, NT, preferred_element_type=jnp.float32)
        delta = jnp.sum(probs * prob_grad, axis=0, keepdims=True)
        score_grad = (probs * (prob_grad - delta)).astype(jnp.bfloat16)

        value_part = lax.dot_general(probs_low, grad, NN, preferred_element_type=jnp.float32)
        key_part = (
            lax.dot_general(score_grad, q_norm, NN, preferred_element_type=jnp.float32)
            * score_scale
        )
        q_grad = (
            lax.dot_general(score_grad, key_norm, TN, preferred_element_type=jnp.float32)
            * score_scale
        )

        scaled = q_gain * q_grad
        inner = jnp.mean(scaled * q_raw, axis=-1, keepdims=True)
        q_out = (
            q_inverse * scaled - q_raw * (q_inverse * q_inverse * q_inverse * inner)
        ).astype(jnp.bfloat16)
        for g, a in enumerate(q_at):
            q_out_ref[:, a] = q_out[g * tokens : (g + 1) * tokens]

        far_key = key_part[:tokens].astype(jnp.bfloat16)
        near_key = key_part[tokens : 2 * tokens].astype(jnp.bfloat16)
        own_key = key_part[2 * tokens :]
        far_out_ref[0, :, at] = far_key
        near_out_ref[0, :, at] = near_key
        key_own_ref[:, at] = own_key
        far_out_ref[1, :, at] = value_part[:tokens].astype(jnp.bfloat16)
        near_out_ref[1, :, at] = value_part[tokens : 2 * tokens].astype(jnp.bfloat16)
        value_own_ref[:, at] = value_part[2 * tokens :]
        key_piece = (
            far_key.astype(jnp.float32) * key_unit[:tokens]
            + near_key.astype(jnp.float32) * key_unit[tokens : 2 * tokens]
            + own_key * key_unit[2 * tokens :]
        )
        return fold_rows(q_grad * q_unit), fold_rows(key_piece)

    pieces = [one_head(head) for head in range(width // HEAD_SIZE)]
    pieces = [sum(p[1:], p[0]) for p in zip(*pieces)]
    pieces = jnp.concatenate([jnp.sum(p, axis=0, keepdims=True) for p in pieces], axis=0)

    @pl.when(step == 0)
    def _():
        gains_ref[...] = pieces

    @pl.when(step != 0)
    def _():
        gains_ref[...] += pieces

    @pl.when(step == pl.num_programs(0) - 1)
    def _():
        terms_ref[...] = jnp.broadcast_to(gains_ref[...][None], terms_ref.shape)


def finish_kernel(
    key_ref, key_own_ref, value_own_ref, near_ref, far_ref, gain_ref, key_out_ref, value_out_ref
):
    gain = gain_ref[...]
    heads = key_ref.shape[1] // HEAD_SIZE
    for h in range(heads):
        at = slice(h * HEAD_SIZE, (h + 1) * HEAD_SIZE)
        total = (
            key_own_ref[:, at]
            + near_ref[0, :, at].astype(jnp.float32)
            + far_ref[0, :, at].astype(jnp.float32)
        )
        raw = key_ref[:, at].astype(jnp.float32)
        inverse = lax.rsqrt(jnp.mean(raw * raw, axis=-1, keepdims=True) + norm_eps)
        scaled = gain * total
        inner = jnp.mean(scaled * raw, axis=-1, keepdims=True)
        key_out_ref[:, at] = (
            inverse * scaled - raw * (inverse * inverse * inverse * inner)
        ).astype(jnp.bfloat16)
    value_out_ref[...] = (
        value_own_ref[...] + near_ref[1].astype(jnp.float32) + far_ref[1].astype(jnp.float32)
    ).astype(jnp.bfloat16)


def spread_kernel(terms_ref, out_ref):
    total = jnp.sum(terms_ref[...], axis=0, keepdims=True)
    out_ref[...] = jnp.broadcast_to(total, out_ref.shape)


def spread(terms, copies):
    return pl.pallas_call(
        spread_kernel,
        out_shape=jax.ShapeDtypeStruct((copies,) + terms.shape[1:], terms.dtype),
        cost_estimate=pl.CostEstimate(
            flops=SPREAD_FLOPS, bytes_accessed=2 * terms.size, transcendentals=0
        ),
        compiler_params=pltpu.CompilerParams(vmem_limit_bytes=1 << 20),
        name="spread_terms",
    )(terms)


def attention(copies, lengths, q_raw, grad, key_raw, values, near, far, q_gain, key_gain):
    tokens, key_width = key_raw.shape
    steps = key_width // (HEAD_SIZE * HEADS_PER_STEP)
    smem = pl.BlockSpec(memory_space=pltpu.SMEM)
    by_head = pl.BlockSpec((tokens, key_width // steps), lambda h: (0, h))
    by_group = pl.BlockSpec((tokens, q_raw.shape[1] // steps), lambda h: (0, h))
    pair = pl.BlockSpec((2, tokens, key_width // steps), lambda h: (0, 0, h))
    row = pl.BlockSpec((1, HEAD_SIZE), lambda h: (0, 0))
    pair_shape = jax.ShapeDtypeStruct((2, tokens, key_width), jnp.bfloat16)
    own_shape = jax.ShapeDtypeStruct((tokens, key_width), jnp.float32)
    return pl.pallas_call(
        attention_kernel,
        grid=(steps,),
        in_specs=[smem, by_group, by_group, by_head, by_head, pair, pair, row, row],
        out_specs=[
            by_group,
            by_head,
            by_head,
            pair,
            pair,
            pl.BlockSpec((copies, 2, HEAD_SIZE), lambda h: (0, 0, 0)),
        ],
        out_shape=[
            jax.ShapeDtypeStruct(q_raw.shape, jnp.bfloat16),
            own_shape,
            own_shape,
            pair_shape,
            pair_shape,
            jax.ShapeDtypeStruct((copies, 2, HEAD_SIZE), jnp.float32),
        ],
        scratch_shapes=[pltpu.VMEM((2, HEAD_SIZE), jnp.float32)],
        cost_estimate=pl.CostEstimate(
            flops=2 * 5 * 3 * tokens * tokens * q_raw.shape[1],
            bytes_accessed=12 * tokens * q_raw.shape[1],
            transcendentals=0,
        ),
        compiler_params=pltpu.CompilerParams(vmem_limit_bytes=VMEM_LIMIT),
        name="window_attention",
    )(lengths, q_raw, grad, key_raw, values, near, far, q_gain, key_gain)


def finish(key_raw, key_own, value_own, near, far, key_gain):
    tokens, key_width = key_raw.shape
    blocks = 4
    wide = key_width // blocks
    flat = pl.BlockSpec((tokens, wide), lambda h: (0, h))
    pair = pl.BlockSpec((2, tokens, wide), lambda h: (0, 0, h))
    row = pl.BlockSpec((1, HEAD_SIZE), lambda h: (0, 0))
    shape = jax.ShapeDtypeStruct((tokens, key_width), jnp.bfloat16)
    return pl.pallas_call(
        finish_kernel,
        grid=(blocks,),
        in_specs=[flat, flat, flat, pair, pair, row],
        out_specs=[flat, flat],
        out_shape=[shape, shape],
        cost_estimate=pl.CostEstimate(
            flops=20 * tokens * key_width,
            bytes_accessed=22 * tokens * key_width,
            transcendentals=0,
        ),
        compiler_params=pltpu.CompilerParams(vmem_limit_bytes=FINISH_LIMIT),
        name="finish_keys",
    )(key_raw, key_own, value_own, near, far, key_gain)


def local(q_raw, key_projection, values, output_gradient, q_gain, key_norm_gain, lengths):
    rows, tokens, query_width = q_raw.shape
    seq_count = lax.axis_size("seq")
    key_raw, value = key_projection[0], values[0]
    key_gain = key_norm_gain.reshape(1, HEAD_SIZE)

    both = jnp.stack([key_raw, value])
    far = shift(both, 2)
    near = shift(both, 1)
    q_out, key_own, value_own, near_part, far_part, terms = attention(
        lax.axis_size("seq"),
        lengths,
        q_raw[0],
        output_gradient[0],
        key_raw,
        value,
        near,
        far,
        q_gain.reshape(1, HEAD_SIZE),
        key_gain,
    )
    terms = lax.all_to_all(terms, "seq", 0, 0)
    far_back = shift(far_part, -2)
    near_back = shift(near_part, -1)
    terms = lax.all_to_all(spread(terms, lax.axis_size("dp")), "dp", 0, 0)
    key_out, value_out = finish(key_raw, key_own, value_own, near_back, far_back, key_gain)
    terms, key_out, value_out = lax.optimization_barrier((terms, key_out, value_out))
    gains = jnp.sum(terms, axis=0)
    token_total = rows * lax.axis_size("dp") * tokens * seq_count
    return (
        q_out[None],
        key_out[None],
        value_out[None],
        gains[0] / math.sqrt(token_total * QUERY_HEADS),
        gains[1] / math.sqrt(token_total * KEY_VALUE_HEADS),
    )


def solution(mesh):
    by_token = P("dp", "seq", None)
    in_specs = (by_token, by_token, by_token, by_token, P(), P(), P("dp", None))
    out_specs = (by_token, by_token, by_token, P(), P())
    return jax.shard_map(local, mesh=mesh, in_specs=in_specs, out_specs=out_specs, check_vma=False)
```

time: 190 us -> 87.3 us (0.46)
  blocking collectives: 144 us -> 0 us
  starting transfers between devices: 17.8 us -> 48.2 us
  waiting for transfers between devices: 8.74 us -> 25.5 us
  Pallas kernels: 13.5 us -> 9.24 us
    psum x1 -> x0, blocking collectives: 144 us -> none  [local(): gains = lax.psum(gains, ('dp', 'seq'))]
    all_to_all x0 -> x2, starting transfers between devices: none -> 35.1 us  [the longest x1 19.4 us: local(): terms = lax.all_to_all(spread(terms, lax.axis_size('dp')), 'dp', 0, 0)]
    all_to_all x0 -> x2, waiting for transfers between devices: none -> 16.7 us  [the longest x1 10.5 us: local(): terms = lax.all_to_all(spread(terms, lax.axis_size('dp')), 'dp', 0, 0)]
    ppermute x4, starting transfers between devices: 17.8 us -> 13 us  [shift(): return lax.ppermute(block, 'seq', route)]
    pallas_call x1 -> x2, Pallas kernels: 9.7 us -> 7.23 us  [the longest x1 6.59 us: attention(): pl.pallas_call(attention_kernel, grid=(steps,), in_specs=[smem, by_group,...]
  transfers between devices with their start and end apart: 4 -> 6, of which waited for: 2 -> 4; matrix products, arithmetic and copies ran while one was open for 0% -> 0% of each run, Pallas kernels for 0% -> 3%
where the time goes in v2:
time: 87.3 us; the launch traced here: 87 us
  starting transfers between devices  48.2 us (55%)
  waiting for transfers between devices  25.5 us (29%)
  Pallas kernels  9.24 us (11%)
  local copies, waits for them, and re-layouts  2.78 us (3%)
    all_to_all x1, starting transfers between devices, local(): terms = lax.all_to_all(spread(terms, lax.axis_size('dp')), 'dp', 0, 0)  19.4 us
    all_to_all x1, starting transfers between devices, local(): terms = lax.all_to_all(terms, 'seq', 0, 0)  15.7 us
    ppermute x4, starting transfers between devices, shift(): return lax.ppermute(block, 'seq', route)  13 us
    all_to_all x1, waiting for transfers between devices, local(): terms = lax.all_to_all(spread(terms, lax.axis_size('dp')), 'dp', 0, 0)  10.5 us
    ppermute x4, waiting for transfers between devices, shift(): return lax.ppermute(block, 'seq', route)  8.75 us
    pallas_call x1, Pallas kernels, attention(): pl.pallas_call(attention_kernel, grid=(steps,), in_specs=[smem, by_group,...  6.59 us
    all_to_all x1, waiting for transfers between devices, local(): terms = lax.all_to_all(terms, 'seq', 0, 0)  6.17 us
    unnamed x15, local copies, waits for them, and re-layouts  2.76 us
  transfers between devices with their start and end apart: 6, of which 4 were waited for; matrix products, arithmetic and copies ran while one was open for 0% of the time, Pallas kernels for 3%

profile of v2, /device:TPU:1, one launch (start us, length us, event | category | flops | bytes accessed | tf_op | source)
XLA Modules:
  0.0 87.0 jit_solution(17888601786902956067)
XLA Ops:
  0.6 0.0 copy-start.1
  0.7 1.0 %constant_dynamic-update-slice_fusion.1 = bf16[2,128,1024]{2,1,0:T(8,128)(2,1)S(1)} fusion(bf16[1,128,1024]{2,1,0:T(8,128)(2,1)} %param.8), kind=kLoop, calls=%fused_computation.1 | loop fusion | bytes 524288
  1.7 0.0 copy-start
  1.7 5.6 %collective-permute-start.1 = (bf16[2,128,1024]{2,1,0:T(8,128)(2,1)S(1)}, bf16[2,128,1024]{2,1,0:T(8,128)(2,1)S(1)}, u32[]{:S(2)}, u32[]{:S(2)}) collective-permute-start(bf16[2,128,1024]{2,1,0:T(8,128)(2,1)S(1)} %constant_dynamic-update-slice_fusion), channel_id=1, source_target_pairs={{0,2},{1,3},{2,4},{3,5},{4,6},{5,7},{6,8},{7,9},{8,10},{9,11},{10,... | collective-permute-start | bytes 1572872 | tf_op jit(solution)/shard_map/ppermute | solution.py:33
  7.4 4.0 %collective-permute-start = (bf16[2,128,1024]{2,1,0:T(8,128)(2,1)S(1)}, bf16[2,128,1024]{2,1,0:T(8,128)(2,1)S(1)}, u32[]{:S(2)}, u32[]{:S(2)}) collective-permute-start(bf16[2,128,1024]{2,1,0:T(8,128)(2,1)S(1)} %constant_dynamic-update-slice_fusion), channel_id=1, source_target_pairs={{0,1},{1,2},{2,3},{3,4},{4,5},{5,6},{6,7},{7,8},{8,9},{9,10},{10,1... | collective-permute-start | bytes 1572872 | tf_op jit(solution)/shard_map/ppermute | solution.py:33
  11.4 2.1 %collective-permute-done.1.far_ref = bf16[2,128,1024]{2,1,0:T(8,128)(2,1)S(1)} collective-permute-done((bf16[2,128,1024]{2,1,0:T(8,128)(2,1)S(1)}, bf16[2,128,1024]{2,1,0:T(8,128)(2,1)S(1)}, u32[]{:S(2)}, u32[]{:S(2)}) %collective-permute-start.1) | collective-permute-done | bytes 524320 | tf_op jit(solution)/shard_map/ppermute | solution.py:33
  13.5 6.6 %collective-permute-done.near_ref = bf16[2,128,1024]{2,1,0:T(8,128)(2,1)S(1)} collective-permute-done((bf16[2,128,1024]{2,1,0:T(8,128)(2,1)S(1)}, bf16[2,128,1024]{2,1,0:T(8,128)(2,1)S(1)}, u32[]{:S(2)}, u32[]{:S(2)}) %collective-permute-start) | collective-permute-done | bytes 524320 | tf_op jit(solution)/shard_map/ppermute | solution.py:33
  20.1 0.0 copy-done.3
  20.1 0.6 copy-done.2
  20.8 0.0 copy-done.5
  20.8 0.0 copy-done.6
  20.8 1.0 %copy-done.4 = bf16[1,128,2048]{2,1,0:T(8,128)(2,1)S(1)} copy-done((bf16[1,128,2048]{2,1,0:T(8,128)(2,1)S(1)}, bf16[1,128,2048]{2,1,0:T(8,128)(2,1)}, u32[]{:S(2)}) %copy-start.4) | copy-done | bytes 524312
  21.8 6.6 %window_attention.1 = (bf16[128,2048]{1,0:T(8,128)(2,1)}, f32[128,1024]{1,0:T(8,128)S(1)}, f32[128,1024]{1,0:T(8,128)S(1)}, bf16[2,128,1024]{2,1,0:T(8,128)(2,1)...) custom-call(s32[1,16]{1,0:T(1,128)S(1)} %copy-done.5, bf16[128,2048]{1,0:T(8,128)(2,1)S(1)} %bitcast.18, ...), custom_call_target="tpu_custom_call" | custom-call | flops 1006632960 | bytes 3145728 | tf_op jit(solution)/shard_map/window_attention/pallas_call | solution.py:209
  28.4 15.7 %all-to-all-start = ((f32[32,2,128]{2,1,0:T(2,128)}), f32[32,2,128]{2,1,0:T(2,128)S(1)}, u32[]{:S(2)}, u32[]{:S(2)}) async-start(f32[32,2,128]{2,1,0:T(2,128)} %get-tuple-element.17), calls=%async_computation | async-start | bytes 65536 | tf_op jit(solution)/shard_map/all_to_all | solution.py:285
  44.1 2.1 %collective-permute-start.2 = (bf16[2,128,1024]{2,1,0:T(8,128)(2,1)S(1)}, bf16[2,128,1024]{2,1,0:T(8,128)(2,1)S(1)}, u32[]{:S(2)}, u32[]{:S(2)}) collective-permute-start(bf16[2,128,1024]{2,1,0:T(8,128)(2,1)S(1)} %get-tuple-element.20), channel_id=1, source_target_pairs={{1,0},{2,1},{3,2},{4,3},{5,4},{6,5},{7,6},{8,7},{9,8},{10,9},{11,1... | collective-permute-start | bytes 1572872 | tf_op jit(solution)/shard_map/ppermute | solution.py:33
  46.3 1.3 %collective-permute-start.3 = (bf16[2,128,1024]{2,1,0:T(8,128)(2,1)S(1)}, bf16[2,128,1024]{2,1,0:T(8,128)(2,1)S(1)}, u32[]{:S(2)}, u32[]{:S(2)}) collective-permute-start(bf16[2,128,1024]{2,1,0:T(8,128)(2,1)S(1)} %get-tuple-element.21), channel_id=1, source_target_pairs={{2,0},{3,1},{4,2},{5,3},{6,4},{7,5},{8,6},{9,7},{10,8},{11,9},{12,... | collective-permute-start | bytes 1572872 | tf_op jit(solution)/shard_map/ppermute | solution.py:33
  47.6 6.2 %all-to-all-done.terms_ref = f32[32,2,128]{2,1,0:T(2,128)S(1)} async-done(((f32[32,2,128]{2,1,0:T(2,128)}), f32[32,2,128]{2,1,0:T(2,128)S(1)}, u32[]{:S(2)}, u32[]{:S(2)}) %all-to-all-start) | async-done | bytes 32800 | tf_op jit(solution)/shard_map/all_to_all | solution.py:285
  53.7 0.6 spread_terms.1
  54.4 19.4 %all-to-all-start.1 = ((f32[32,2,128]{2,1,0:T(2,128)}), f32[32,2,128]{2,1,0:T(2,128)S(1)}, u32[]{:S(2)}, u32[]{:S(2)}) async-start(f32[32,2,128]{2,1,0:T(2,128)} %spread_terms.1), calls=%async_computation.1 | async-start | bytes 65536 | tf_op jit(solution)/shard_map/all_to_all | solution.py:288
  73.8 0.0 collective-permute-done.2.near_ref
  73.8 0.0 collective-permute-done.3.far_ref
  73.8 2.0 %finish_keys.1 = (bf16[128,1024]{1,0:T(8,128)(2,1)}, bf16[128,1024]{1,0:T(8,128)(2,1)}) custom-call(bf16[128,1024]{1,0:T(8,128)(2,1)S(1)} %bitcast.14, f32[128,1024]{1,0:T(8,128)S(1)} %get-tuple-element.18.key_own_ref, f32[128,1024]{1,0:T(8,128)S(1)} %get-tuple-element.19.value_own_ref, bf16[2,128,1024]{2,1,0:T(8,128)(2,1)S(1)} %collective-permute-done.2.near_ref, ...), custom_call_target="tpu_custom_call" | custom-call | flops 2621440 | bytes 2883584 | tf_op jit(solution)/shard_map/finish_keys/pallas_call | solution.py:248
  75.9 10.5 %all-to-all-done.1 = f32[32,2,128]{2,1,0:T(2,128)S(1)} async-done(((f32[32,2,128]{2,1,0:T(2,128)}), f32[32,2,128]{2,1,0:T(2,128)S(1)}, u32[]{:S(2)}, u32[]{:S(2)}) %all-to-all-start.1) | async-done | bytes 32800 | tf_op jit(solution)/shard_map/all_to_all | solution.py:288
  86.4 0.5 multiply_bitcast_fusion
  (9 shorter events, 0.1 us)
Async XLA Ops:
  0.6 1.1 %copy-start.1 = (bf16[1,128,1024]{2,1,0:T(8,128)(2,1)S(1)}, bf16[1,128,1024]{2,1,0:T(8,128)(2,1)}, u32[]{:S(2)}) copy-start(bf16[1,128,1024]{2,1,0:T(8,128)(2,1)} %param.9) | copy-start | bytes 786436
  0.6 19.5 %copy-start.3 = (bf16[1,128,2048]{2,1,0:T(8,128)(2,1)S(1)}, bf16[1,128,2048]{2,1,0:T(8,128)(2,1)}, u32[]{:S(2)}) copy-start(bf16[1,128,2048]{2,1,0:T(8,128)(2,1)} %param.7) | copy-start | bytes 1572868
  1.7 18.4 %copy-start = (bf16[1,128,1024]{2,1,0:T(8,128)(2,1)S(1)}, bf16[1,128,1024]{2,1,0:T(8,128)(2,1)}, u32[]{:S(2)}) copy-start(bf16[1,128,1024]{2,1,0:T(8,128)(2,1)} %param.8) | copy-start | bytes 786436
  1.7 11.7 %collective-permute-start.1 = (bf16[2,128,1024]{2,1,0:T(8,128)(2,1)S(1)}, bf16[2,128,1024]{2,1,0:T(8,128)(2,1)S(1)}, u32[]{:S(2)}, u32[]{:S(2)}) collective-permute-start(bf16[2,128,1024]{2,1,0:T(8,128)(2,1)S(1)} %constant_dynamic-update-slice_fusion), channel_id=1, source_target_pairs={{0,2},{1,3},{2,4},{3,5},{4,6},{5,7},{6,8},{7,9},{8,10},{9,11},{10,... | collective-permute-start | bytes 1572872 | tf_op jit(solution)/shard_map/ppermute | solution.py:33
  7.4 12.7 %collective-permute-start = (bf16[2,128,1024]{2,1,0:T(8,128)(2,1)S(1)}, bf16[2,128,1024]{2,1,0:T(8,128)(2,1)S(1)}, u32[]{:S(2)}, u32[]{:S(2)}) collective-permute-start(bf16[2,128,1024]{2,1,0:T(8,128)(2,1)S(1)} %constant_dynamic-update-slice_fusion), channel_id=1, source_target_pairs={{0,1},{1,2},{2,3},{3,4},{4,5},{5,6},{6,7},{7,8},{8,9},{9,10},{10,1... | collective-permute-start | bytes 1572872 | tf_op jit(solution)/shard_map/ppermute | solution.py:33
  20.1 0.7 copy-start.2
  20.1 0.7 copy-start.5
  20.1 0.7 copy-start.6
  20.8 1.0 %copy-start.4 = (bf16[1,128,2048]{2,1,0:T(8,128)(2,1)S(1)}, bf16[1,128,2048]{2,1,0:T(8,128)(2,1)}, u32[]{:S(2)}) copy-start(bf16[1,128,2048]{2,1,0:T(8,128)(2,1)} %param.10) | copy-start | bytes 1572868
  28.4 25.3 %all-to-all-start = ((f32[32,2,128]{2,1,0:T(2,128)}), f32[32,2,128]{2,1,0:T(2,128)S(1)}, u32[]{:S(2)}, u32[]{:S(2)}) async-start(f32[32,2,128]{2,1,0:T(2,128)} %get-tuple-element.17), calls=%async_computation | async-start | bytes 65536 | tf_op jit(solution)/shard_map/all_to_all | solution.py:285
  44.1 29.7 %collective-permute-start.2 = (bf16[2,128,1024]{2,1,0:T(8,128)(2,1)S(1)}, bf16[2,128,1024]{2,1,0:T(8,128)(2,1)S(1)}, u32[]{:S(2)}, u32[]{:S(2)}) collective-permute-start(bf16[2,128,1024]{2,1,0:T(8,128)(2,1)S(1)} %get-tuple-element.20), channel_id=1, source_target_pairs={{1,0},{2,1},{3,2},{4,3},{5,4},{6,5},{7,6},{8,7},{9,8},{10,9},{11,1... | collective-permute-start | bytes 1572872 | tf_op jit(solution)/shard_map/ppermute | solution.py:33
  46.3 27.6 %collective-permute-start.3 = (bf16[2,128,1024]{2,1,0:T(8,128)(2,1)S(1)}, bf16[2,128,1024]{2,1,0:T(8,128)(2,1)S(1)}, u32[]{:S(2)}, u32[]{:S(2)}) collective-permute-start(bf16[2,128,1024]{2,1,0:T(8,128)(2,1)S(1)} %get-tuple-element.21), channel_id=1, source_target_pairs={{2,0},{3,1},{4,2},{5,3},{6,4},{7,5},{8,6},{9,7},{10,8},{11,9},{12,... | collective-permute-start | bytes 1572872 | tf_op jit(solution)/shard_map/ppermute | solution.py:33
  54.4 32.0 %all-to-all-start.1 = ((f32[32,2,128]{2,1,0:T(2,128)}), f32[32,2,128]{2,1,0:T(2,128)S(1)}, u32[]{:S(2)}, u32[]{:S(2)}) async-start(f32[32,2,128]{2,1,0:T(2,128)} %spread_terms.1), calls=%async_computation.1 | async-start | bytes 65536 | tf_op jit(solution)/shard_map/all_to_all | solution.py:288

commit v3 on v2

--- a/solution.py
+++ b/solution.py
@@ -33,6 +33,12 @@
     return lax.ppermute(block, "seq", route)
 
 
+def behind(block, distant):
+    count = lax.axis_size("seq")
+    odd = lax.axis_index("seq") % 2 == 1
+    return lax.ppermute(jnp.where(odd, distant, block), "seq", [(i, i ^ 1) for i in range(count)])
+
+
 def fold_rows(x):
     return jnp.sum(x.reshape(-1, 8, x.shape[-1]), axis=0)
 
@@ -43,8 +49,10 @@
     grad_ref,
     key_ref,
     value_ref,
-    near_ref,
-    far_ref,
+    near_key_ref,
+    near_value_ref,
+    far_key_ref,
+    far_value_ref,
     q_gain_ref,
     key_gain_ref,
     q_out_ref,
@@ -87,12 +95,14 @@
         q_norm = (q_unit * q_gain).astype(jnp.bfloat16)
         grad = jnp.concatenate([grad_ref[:, a] for a in q_at], axis=0)
         key_raw = jnp.concatenate(
-            [far_ref[0, :, at], near_ref[0, :, at], key_ref[:, at]], axis=0
+            [far_key_ref[:, at], near_key_ref[:, at], key_ref[:, at]], axis=0
         ).astype(jnp.float32)
         key_inverse = lax.rsqrt(jnp.mean(key_raw * key_raw, axis=-1, keepdims=True) + norm_eps)
         key_unit = key_raw * key_inverse
         key_norm = (key_unit * key_gain).astype(jnp.bfloat16)
-        values = jnp.concatenate([far_ref[1, :, at], near_ref[1, :, at], value_ref[:, at]], axis=0)
+        values = jnp.concatenate(
+            [far_value_ref[:, at], near_value_ref[:, at], value_ref[:, at]], axis=0
+        )
 
         scores = lax.dot_general(key_norm, q_norm, NT, preferred_element_type=jnp.float32)
         scores = jnp.where(allowed, scores, jnp.float32(-1e30))
@@ -196,7 +206,7 @@
     )(terms)
 
 
-def attention(copies, lengths, q_raw, grad, key_raw, values, near, far, q_gain, key_gain):
+def attention(copies, lengths, q_raw, grad, key_raw, values, near, far, gains):
     tokens, key_width = key_raw.shape
     steps = key_width // (HEAD_SIZE * HEADS_PER_STEP)
     smem = pl.BlockSpec(memory_space=pltpu.SMEM)
@@ -209,7 +219,7 @@
     return pl.pallas_call(
         attention_kernel,
         grid=(steps,),
-        in_specs=[smem, by_group, by_group, by_head, by_head, pair, pair, row, row],
+        in_specs=[smem, by_group, by_group] + [by_head] * 6 + [row, row],
         out_specs=[
             by_group,
             by_head,
@@ -234,7 +244,7 @@
         ),
         compiler_params=pltpu.CompilerParams(vmem_limit_bytes=VMEM_LIMIT),
         name="window_attention",
-    )(lengths, q_raw, grad, key_raw, values, near, far, q_gain, key_gain)
+    )(lengths, q_raw, grad, key_raw, values, *near, *far, *gains)
 
 
 def finish(key_raw, key_own, value_own, near, far, key_gain):
@@ -267,9 +277,8 @@
     key_raw, value = key_projection[0], values[0]
     key_gain = key_norm_gain.reshape(1, HEAD_SIZE)
 
-    both = jnp.stack([key_raw, value])
-    far = shift(both, 2)
-    near = shift(both, 1)
+    far = [shift(block, 2) for block in (key_raw, value)]
+    near = [behind(block, distant) for block, distant in zip((key_raw, value), far)]
     q_out, key_own, value_own, near_part, far_part, terms = attention(
         lax.axis_size("seq"),
         lengths,
@@ -279,8 +288,7 @@
         value,
         near,
         far,
-        q_gain.reshape(1, HEAD_SIZE),
-        key_gain,
+        (q_gain.reshape(1, HEAD_SIZE), key_gain),
     )
     terms = lax.all_to_all(terms, "seq", 0, 0)
     far_back = shift(far_part, -2)

time: 87.3 us -> 83.2 us (0.953)
  waiting for transfers between devices: 25.5 us -> 18.6 us
  starting transfers between devices: 48.2 us -> 51.7 us
  local copies, waits for them, and re-layouts: 2.78 us -> 0.68 us
  other arithmetic: 0.56 us -> 1.63 us
    ppermute x0 -> x2, starting transfers between devices: none -> 14.5 us  [behind(): lax.ppermute(jnp.where(odd, distant, block), 'seq', [(i, i ^ 1) for i in...]
    all_to_all x1, starting transfers between devices: 15.7 us -> 5.71 us  [local(): terms = lax.all_to_all(terms, 'seq', 0, 0)]
    ppermute x4, waiting for transfers between devices: 8.75 us -> 0.43 us  [shift(): return lax.ppermute(block, 'seq', route)]
    unnamed x15 -> x14, local copies, waits for them, and re-layouts: 2.76 us -> 0.68 us
    ppermute x0 -> x2, waiting for transfers between devices: none -> 1.49 us  [behind(): lax.ppermute(jnp.where(odd, distant, block), 'seq', [(i, i ^ 1) for i in...]
    select_n x0 -> x2, other arithmetic: none -> 1.07 us  [behind(): jnp.where(odd, distant, block)]
    ppermute x4, starting transfers between devices: 13 us -> 12.1 us  [shift(): return lax.ppermute(block, 'seq', route)]
  transfers between devices with their start and end apart: 6 -> 8, of which waited for: 4 -> 4; matrix products, arithmetic and copies ran while one was open for 0% -> 1% of each run, Pallas kernels for 3% -> 3%
where the time goes in v3:
time: 83.2 us; the launch traced here: 82.8 us
  starting transfers between devices  51.7 us (62%)
  waiting for transfers between devices  18.6 us (22%)
  Pallas kernels  9.27 us (11%)
  other arithmetic  1.63 us (2%)
    all_to_all x1, starting transfers between devices, local(): terms = lax.all_to_all(spread(terms, lax.axis_size('dp')), 'dp', 0, 0)  19.4 us
    ppermute x2, starting transfers between devices, behind(): lax.ppermute(jnp.where(odd, distant, block), 'seq', [(i, i ^ 1) for i in...  14.5 us
    ppermute x4, starting transfers between devices, shift(): return lax.ppermute(block, 'seq', route)  12.1 us
    all_to_all x1, waiting for transfers between devices, local(): terms = lax.all_to_all(spread(terms, lax.axis_size('dp')), 'dp', 0, 0)  10.5 us
    pallas_call x1, Pallas kernels, attention(): pl.pallas_call(attention_kernel, grid=(steps,), in_specs=[smem, by_group,...  6.61 us
    all_to_all x1, waiting for transfers between devices, local(): terms = lax.all_to_all(terms, 'seq', 0, 0)  6.17 us
    all_to_all x1, starting transfers between devices, local(): terms = lax.all_to_all(terms, 'seq', 0, 0)  5.71 us
    pallas_call x1, Pallas kernels, finish(): pl.pallas_call(finish_kernel, grid=(blocks,), in_specs=[flat, flat, flat,...  2.02 us
  transfers between devices with their start and end apart: 8, of which 4 were waited for; matrix products, arithmetic and copies ran while one was open for 1% of the time, Pallas kernels for 3%

profile of v3, /device:TPU:1, one launch (start us, length us, event | category | flops | bytes accessed | tf_op | source)
XLA Modules:
  0.0 82.8 jit_solution(15943574142446733416)
XLA Ops:
  0.6 5.5 %collective-permute-start = (bf16[128,1024]{1,0:T(8,128)(2,1)}, bf16[128,1024]{1,0:T(8,128)(2,1)S(1)}, u32[]{:S(2)}, u32[]{:S(2)}) collective-permute-start(bf16[128,1024]{1,0:T(8,128)(2,1)} %bitcast.15), channel_id=1, source_target_pairs={{0,2},{1,3},{2,4},{3,5},{4,6},{5,7},{6,8},{7,9},{8,10},{9,11},{10,... | collective-permute-start | bytes 786440 | tf_op jit(solution)/shard_map/ppermute | solution.py:33
  6.1 3.1 %collective-permute-start.2 = (bf16[128,1024]{1,0:T(8,128)(2,1)}, bf16[128,1024]{1,0:T(8,128)(2,1)S(1)}, u32[]{:S(2)}, u32[]{:S(2)}) collective-permute-start(bf16[128,1024]{1,0:T(8,128)(2,1)} %bitcast.18), channel_id=1, source_target_pairs={{0,2},{1,3},{2,4},{3,5},{4,6},{5,7},{6,8},{7,9},{8,10},{9,11},{10,... | collective-permute-start | bytes 786440 | tf_op jit(solution)/shard_map/ppermute | solution.py:33
  9.3 0.4 collective-permute-done.far_key_ref
  9.7 1.0 %broadcast_select_fusion.1 = bf16[128,1024]{1,0:T(8,128)(2,1)S(1)} fusion(bf16[128,1024]{1,0:T(8,128)(2,1)S(1)} %collective-permute-done.far_key_ref, pred[]{:T(512)S(6)} %eq.7, bf16[1,128,1024]{2,1,0:T(8,128)(2,1)} %param.8), kind=kLoop, calls=%fused_computation.1 | loop fusion | flops 131072 | bytes 786433 | tf_op jit(solution)/shard_map/jit(_where)/select_n | solution.py:39
  10.8 0.0 copy-start
  10.8 0.0 copy-start.3
  10.8 12.6 %collective-permute-start.1 = (bf16[128,1024]{1,0:T(8,128)(2,1)S(1)}, bf16[128,1024]{1,0:T(8,128)(2,1)S(1)}, u32[]{:S(2)}, u32[]{:S(2)}) collective-permute-start(bf16[128,1024]{1,0:T(8,128)(2,1)S(1)} %broadcast_select_fusion.1), channel_id=1, source_target_pairs={{0,1},{1,0},{2,3},{3,2},{4,5},{5,4},{6,7},{7,6},{8,9},{9,8},{10,11... | collective-permute-start | bytes 786440 | tf_op jit(solution)/shard_map/ppermute | solution.py:39
  23.4 1.9 %collective-permute-start.3 = (bf16[128,1024]{1,0:T(8,128)(2,1)S(1)}, bf16[128,1024]{1,0:T(8,128)(2,1)S(1)}, u32[]{:S(2)}, u32[]{:S(2)}) collective-permute-start(bf16[128,1024]{1,0:T(8,128)(2,1)S(1)} %broadcast_select_fusion), channel_id=1, source_target_pairs={{0,1},{1,0},{2,3},{3,2},{4,5},{5,4},{6,7},{7,6},{8,9},{9,8},{10,11... | collective-permute-start | bytes 786440 | tf_op jit(solution)/shard_map/ppermute | solution.py:39
  25.4 0.0 collective-permute-done.1.near_key_ref
  25.4 1.5 %collective-permute-done.3.near_value_ref = bf16[128,1024]{1,0:T(8,128)(2,1)S(1)} collective-permute-done((bf16[128,1024]{1,0:T(8,128)(2,1)S(1)}, bf16[128,1024]{1,0:T(8,128)(2,1)S(1)}, u32[]{:S(2)}, u32[]{:S(2)}) %collective-permute-start.3) | collective-permute-done | bytes 262176 | tf_op jit(solution)/shard_map/ppermute | solution.py:39
  26.9 0.6 copy-done.2
  27.5 0.0 copy-done.5
  27.6 0.0 copy-done.6
  27.6 6.6 %window_attention.1 = (bf16[128,2048]{1,0:T(8,128)(2,1)}, f32[128,1024]{1,0:T(8,128)S(1)}, f32[128,1024]{1,0:T(8,128)S(1)}, bf16[2,128,1024]{2,1,0:T(8,128)(2,1)...) custom-call(s32[1,16]{1,0:T(1,128)S(1)} %copy-done.5, bf16[128,2048]{1,0:T(8,128)(2,1)S(1)} %bitcast.22, ...), custom_call_target="tpu_custom_call" | custom-call | flops 1006632960 | bytes 3145728 | tf_op jit(solution)/shard_map/window_attention/pallas_call | solution.py:219
  34.2 5.7 %all-to-all-start = ((f32[32,2,128]{2,1,0:T(2,128)}), f32[32,2,128]{2,1,0:T(2,128)S(1)}, u32[]{:S(2)}, u32[]{:S(2)}) async-start(f32[32,2,128]{2,1,0:T(2,128)} %get-tuple-element.17), calls=%async_computation | async-start | bytes 65536 | tf_op jit(solution)/shard_map/all_to_all | solution.py:293
  39.9 2.1 %collective-permute-start.4 = (bf16[2,128,1024]{2,1,0:T(8,128)(2,1)S(1)}, bf16[2,128,1024]{2,1,0:T(8,128)(2,1)S(1)}, u32[]{:S(2)}, u32[]{:S(2)}) collective-permute-start(bf16[2,128,1024]{2,1,0:T(8,128)(2,1)S(1)} %get-tuple-element.20), channel_id=1, source_target_pairs={{1,0},{2,1},{3,2},{4,3},{5,4},{6,5},{7,6},{8,7},{9,8},{10,9},{11,1... | collective-permute-start | bytes 1572872 | tf_op jit(solution)/shard_map/ppermute | solution.py:33
  42.0 1.3 %collective-permute-start.5 = (bf16[2,128,1024]{2,1,0:T(8,128)(2,1)S(1)}, bf16[2,128,1024]{2,1,0:T(8,128)(2,1)S(1)}, u32[]{:S(2)}, u32[]{:S(2)}) collective-permute-start(bf16[2,128,1024]{2,1,0:T(8,128)(2,1)S(1)} %get-tuple-element.21), channel_id=1, source_target_pairs={{2,0},{3,1},{4,2},{5,3},{6,4},{7,5},{8,6},{9,7},{10,8},{11,9},{12,... | collective-permute-start | bytes 1572872 | tf_op jit(solution)/shard_map/ppermute | solution.py:33
  43.3 6.2 %all-to-all-done.terms_ref = f32[32,2,128]{2,1,0:T(2,128)S(1)} async-done(((f32[32,2,128]{2,1,0:T(2,128)}), f32[32,2,128]{2,1,0:T(2,128)S(1)}, u32[]{:S(2)}, u32[]{:S(2)}) %all-to-all-start) | async-done | bytes 32800 | tf_op jit(solution)/shard_map/all_to_all | solution.py:293
  49.5 0.6 spread_terms.1
  50.2 19.4 %all-to-all-start.1 = ((f32[32,2,128]{2,1,0:T(2,128)}), f32[32,2,128]{2,1,0:T(2,128)S(1)}, u32[]{:S(2)}, u32[]{:S(2)}) async-start(f32[32,2,128]{2,1,0:T(2,128)} %spread_terms.1), calls=%async_computation.1 | async-start | bytes 65536 | tf_op jit(solution)/shard_map/all_to_all | solution.py:296
  69.6 0.0 collective-permute-done.5.far_ref
  69.6 2.0 %finish_keys.1 = (bf16[128,1024]{1,0:T(8,128)(2,1)}, bf16[128,1024]{1,0:T(8,128)(2,1)}) custom-call(bf16[128,1024]{1,0:T(8,128)(2,1)S(1)} %bitcast.17, f32[128,1024]{1,0:T(8,128)S(1)} %get-tuple-element.18.key_own_ref, f32[128,1024]{1,0:T(8,128)S(1)} %get-tuple-element.19.value_own_ref, bf16[2,128,1024]{2,1,0:T(8,128)(2,1)S(1)} %collective-permute-done.4.near_ref, ...), custom_call_target="tpu_custom_call" | custom-call | flops 2621440 | bytes 2883584 | tf_op jit(solution)/shard_map/finish_keys/pallas_call | solution.py:258
  71.7 10.5 %all-to-all-done.1 = f32[32,2,128]{2,1,0:T(2,128)S(1)} async-done(((f32[32,2,128]{2,1,0:T(2,128)}), f32[32,2,128]{2,1,0:T(2,128)S(1)}, u32[]{:S(2)}, u32[]{:S(2)}) %all-to-all-start.1) | async-done | bytes 32800 | tf_op jit(solution)/shard_map/all_to_all | solution.py:296
  82.2 0.5 multiply_bitcast_fusion
  (13 shorter events, 0.1 us)
Async XLA Ops:
  0.6 9.1 %collective-permute-start = (bf16[128,1024]{1,0:T(8,128)(2,1)}, bf16[128,1024]{1,0:T(8,128)(2,1)S(1)}, u32[]{:S(2)}, u32[]{:S(2)}) collective-permute-start(bf16[128,1024]{1,0:T(8,128)(2,1)} %bitcast.15), channel_id=1, source_target_pairs={{0,2},{1,3},{2,4},{3,5},{4,6},{5,7},{6,8},{7,9},{8,10},{9,11},{10,... | collective-permute-start | bytes 786440 | tf_op jit(solution)/shard_map/ppermute | solution.py:33
  6.1 17.3 %collective-permute-start.2 = (bf16[128,1024]{1,0:T(8,128)(2,1)}, bf16[128,1024]{1,0:T(8,128)(2,1)S(1)}, u32[]{:S(2)}, u32[]{:S(2)}) collective-permute-start(bf16[128,1024]{1,0:T(8,128)(2,1)} %bitcast.18), channel_id=1, source_target_pairs={{0,2},{1,3},{2,4},{3,5},{4,6},{5,7},{6,8},{7,9},{8,10},{9,11},{10,... | collective-permute-start | bytes 786440 | tf_op jit(solution)/shard_map/ppermute | solution.py:33
  9.3 14.1 %copy-start.1 = (bf16[1,128,1024]{2,1,0:T(8,128)(2,1)S(1)}, bf16[1,128,1024]{2,1,0:T(8,128)(2,1)}, u32[]{:S(2)}) copy-start(bf16[1,128,1024]{2,1,0:T(8,128)(2,1)} %param.9) | copy-start | bytes 786436
  9.7 17.2 %copy-start.4 = (bf16[1,128,2048]{2,1,0:T(8,128)(2,1)S(1)}, bf16[1,128,2048]{2,1,0:T(8,128)(2,1)}, u32[]{:S(2)}) copy-start(bf16[1,128,2048]{2,1,0:T(8,128)(2,1)} %param.10) | copy-start | bytes 1572868
  10.8 16.1 %copy-start = (bf16[1,128,1024]{2,1,0:T(8,128)(2,1)S(1)}, bf16[1,128,1024]{2,1,0:T(8,128)(2,1)}, u32[]{:S(2)}) copy-start(bf16[1,128,1024]{2,1,0:T(8,128)(2,1)} %param.8) | copy-start | bytes 786436
  10.8 16.1 %copy-start.3 = (bf16[1,128,2048]{2,1,0:T(8,128)(2,1)S(1)}, bf16[1,128,2048]{2,1,0:T(8,128)(2,1)}, u32[]{:S(2)}) copy-start(bf16[1,128,2048]{2,1,0:T(8,128)(2,1)} %param.7) | copy-start | bytes 1572868
  10.8 14.6 %collective-permute-start.1 = (bf16[128,1024]{1,0:T(8,128)(2,1)S(1)}, bf16[128,1024]{1,0:T(8,128)(2,1)S(1)}, u32[]{:S(2)}, u32[]{:S(2)}) collective-permute-start(bf16[128,1024]{1,0:T(8,128)(2,1)S(1)} %broadcast_select_fusion.1), channel_id=1, source_target_pairs={{0,1},{1,0},{2,3},{3,2},{4,5},{5,4},{6,7},{7,6},{8,9},{9,8},{10,11... | collective-permute-start | bytes 786440 | tf_op jit(solution)/shard_map/ppermute | solution.py:39
  23.4 3.4 %collective-permute-start.3 = (bf16[128,1024]{1,0:T(8,128)(2,1)S(1)}, bf16[128,1024]{1,0:T(8,128)(2,1)S(1)}, u32[]{:S(2)}, u32[]{:S(2)}) collective-permute-start(bf16[128,1024]{1,0:T(8,128)(2,1)S(1)} %broadcast_select_fusion), channel_id=1, source_target_pairs={{0,1},{1,0},{2,3},{3,2},{4,5},{5,4},{6,7},{7,6},{8,9},{9,8},{10,11... | collective-permute-start | bytes 786440 | tf_op jit(solution)/shard_map/ppermute | solution.py:39
  26.9 0.7 copy-start.2
  26.9 0.7 copy-start.5
  26.9 0.7 copy-start.6
  34.2 15.3 %all-to-all-start = ((f32[32,2,128]{2,1,0:T(2,128)}), f32[32,2,128]{2,1,0:T(2,128)S(1)}, u32[]{:S(2)}, u32[]{:S(2)}) async-start(f32[32,2,128]{2,1,0:T(2,128)} %get-tuple-element.17), calls=%async_computation | async-start | bytes 65536 | tf_op jit(solution)/shard_map/all_to_all | solution.py:293
  39.9 29.7 %collective-permute-start.4 = (bf16[2,128,1024]{2,1,0:T(8,128)(2,1)S(1)}, bf16[2,128,1024]{2,1,0:T(8,128)(2,1)S(1)}, u32[]{:S(2)}, u32[]{:S(2)}) collective-permute-start(bf16[2,128,1024]{2,1,0:T(8,128)(2,1)S(1)} %get-tuple-element.20), channel_id=1, source_target_pairs={{1,0},{2,1},{3,2},{4,3},{5,4},{6,5},{7,6},{8,7},{9,8},{10,9},{11,1... | collective-permute-start | bytes 1572872 | tf_op jit(solution)/shard_map/ppermute | solution.py:33
  42.0 27.6 %collective-permute-start.5 = (bf16[2,128,1024]{2,1,0:T(8,128)(2,1)S(1)}, bf16[2,128,1024]{2,1,0:T(8,128)(2,1)S(1)}, u32[]{:S(2)}, u32[]{:S(2)}) collective-permute-start(bf16[2,128,1024]{2,1,0:T(8,128)(2,1)S(1)} %get-tuple-element.21), channel_id=1, source_target_pairs={{2,0},{3,1},{4,2},{5,3},{6,4},{7,5},{8,6},{9,7},{10,8},{11,9},{12,... | collective-permute-start | bytes 1572872 | tf_op jit(solution)/shard_map/ppermute | solution.py:33
  50.2 32.0 %all-to-all-start.1 = ((f32[32,2,128]{2,1,0:T(2,128)}), f32[32,2,128]{2,1,0:T(2,128)S(1)}, u32[]{:S(2)}, u32[]{:S(2)}) async-start(f32[32,2,128]{2,1,0:T(2,128)} %spread_terms.1), calls=%async_computation.1 | async-start | bytes 65536 | tf_op jit(solution)/shard_map/all_to_all | solution.py:296
